TPU v7x, 32 devices: a whole 2x2x4 slice. The times are simulated.
32 devices in a mesh: seq: 8 (over z, y), ch: 4 (over x, core).
Axes of the slice: x: 2, y: 2, z: 4, core: 2. Of those that a mesh axis runs over, the one named last changes fastest.
Arguments:
- queries: float32 [1024, 1024], P('seq', 'ch'), may hold values from -6 to 6
- keys: float32 [1024, 1024], P('seq', 'ch'), may hold values from -6 to 6
- values: float32 [1024, 1024], P('seq', 'ch'), may hold values from -6 to 6
- filters: float32 [1024, 1024], P('seq', 'ch'), may hold values from -0.375 to 0.375
- short_w: float32 [3, 1024], P(None, 'ch'), may hold values from -3.5 to 3.5
- bias: float32 [1024], P('ch'), may hold values from -4 to 4
Outputs:
- mixed: float32 [1024, 1024], P('seq', 'ch')
All inputs are finite; a program needn't handle non-finite values.
Results may differ from a plain program's by a relative error of at most 0.00011.
Values sent between devices are 32-bit elements; how exact they have to be, the bound alone decides.
A program may use at most 64 MiB of HBM per device.

v0:
```python
import math
import jax
import jax.numpy as jnp
from jax import lax
from jax.sharding import PartitionSpec as P


def passed_along(block, axis, distance):
    devices = range(lax.axis_size(axis))
    route = [(i - distance, i) for i in devices if i - distance in devices]
    return lax.ppermute(block, axis, route)


def angles(index, modulus, sign):
    turned = (index % modulus).astype(jnp.float32) * (2.0 * math.pi / modulus)
    return (jnp.cos(turned), sign * jnp.sin(turned))


def complex_mix(form, mat_real, mat_imag, data_real, data_imag):
    first = jnp.einsum(form, mat_real, data_real, precision=lax.Precision.HIGHEST)
    second = jnp.einsum(form, mat_imag, data_imag, precision=lax.Precision.HIGHEST)
    third = jnp.einsum(form, mat_real, data_imag, precision=lax.Precision.HIGHEST)
    fourth = jnp.einsum(form, mat_imag, data_real, precision=lax.Precision.HIGHEST)
    return (first - second, third + fourth)


def body(queries, keys, values, filters, short_w, bias):
    row_count, channels = queries.shape
    shards = lax.axis_size("seq")
    device = lax.axis_index("seq")
    slab = row_count // shards
    total = row_count * shards
    stacked = jnp.stack((queries, keys, values))
    earlier = passed_along(stacked[:, row_count - 2 :, :], "seq", 1)
    extended = jnp.concatenate((earlier, stacked), axis=1)
    shorted = (
        short_w[0] * extended[:, 2:]
        + short_w[1] * extended[:, 1:-1]
        + short_w[2] * extended[:, :-2]
    )
    gated = shorted[1] * shorted[2]
    signal = jnp.stack((gated, filters))
    within = device * slab + jnp.arange(slab, dtype=jnp.int32)
    column_index = jnp.arange(shards, dtype=jnp.int32)
    row_index = jnp.arange(row_count, dtype=jnp.int32)
    own_pos = row_count * device + row_index
    cosine, sine = angles(own_pos, 2 * total, -1.0)
    lifted = jnp.stack((signal, signal * cosine[:, None], signal * sine[:, None]), axis=1)[
        :, :, None
    ]
    received = lax.all_to_all(lifted, "seq", split_axis=3, concat_axis=2, tiled=True)
    real_part = jnp.stack((received[:, 0], received[:, 1]), axis=1)
    imag_part = jnp.stack((jnp.zeros_like(received[:, 0]), received[:, 2]), axis=1)
    freq_cos, freq_sin = angles(column_index[:, None] * column_index[None, :], shards, -1.0)
    real_part, imag_part = complex_mix("kd,srdmc->srkmc", freq_cos, freq_sin, real_part, imag_part)
    twist_cos, twist_sin = angles(column_index[:, None] * within[None, :], total, -1.0)
    twist_cos = twist_cos[:, :, None]
    twist_sin = twist_sin[:, :, None]
    real_part, imag_part = (
        real_part * twist_cos - imag_part * twist_sin,
        real_part * twist_sin + imag_part * twist_cos,
    )
    square_index = row_index[:, None] * row_index[None, :]
    long_cos, long_sin = angles(square_index, row_count, -1.0)
    pair = (
        lax.all_to_all(real_part, "seq", split_axis=2, concat_axis=3, tiled=True),
        lax.all_to_all(imag_part, "seq", split_axis=2, concat_axis=3, tiled=True),
    )
    spec_real, spec_imag = complex_mix("km,srjmc->srjkc", long_cos, long_sin, pair[0], pair[1])
    prod_real = spec_real[0] * spec_real[1] - spec_imag[0] * spec_imag[1]
    prod_imag = spec_real[0] * spec_imag[1] + spec_imag[0] * spec_real[1]
    inverse_cos, inverse_sin = angles(square_index, row_count, 1.0)
    back_real, back_imag = complex_mix(
        "mk,rjkc->rjmc", inverse_cos, inverse_sin, prod_real, prod_imag
    )
    undo_cos, undo_sin = angles(device * row_index, total, 1.0)
    undo_cos = undo_cos[:, None]
    undo_sin = undo_sin[:, None]
    back_real, back_imag = (
        back_real * undo_cos - back_imag * undo_sin,
        back_real * undo_sin + back_imag * undo_cos,
    )
    column_cos, column_sin = angles(column_index[:, None] * column_index[None, :], shards, 1.0)
    pair = (
        lax.all_to_all(back_real, "seq", split_axis=2, concat_axis=1, tiled=True),
        lax.all_to_all(back_imag, "seq", split_axis=2, concat_axis=1, tiled=True),
    )
    inv_real, inv_imag = complex_mix("dk,rkmc->rdmc", column_cos, column_sin, pair[0], pair[1])
    factor = 0.5 / total
    packed = jnp.stack((inv_real[0], inv_imag[0], inv_real[1], inv_imag[1]))
    landed = lax.all_to_all(packed, "seq", split_axis=1, concat_axis=2, tiled=True)
    cosine, sine = angles(own_pos, 2 * total, 1.0)
    long_part = factor * (
        landed[0, 0] + cosine[:, None] * landed[2, 0] - sine[:, None] * landed[3, 0]
    )
    return shorted[0] * (long_part + bias * gated)


def solution(mesh):
    placed = (
        P("seq", "ch"),
        P("seq", "ch"),
        P("seq", "ch"),
        P("seq", "ch"),
        P(None, "ch"),
        P("ch"),
    )
    return jax.shard_map(
        body, mesh=mesh, in_specs=placed, out_specs=P("seq", "ch"), check_vma=False
    )
```

profile of v0, /device:TPU:0, one launch (start us, length us, event | category | flops | bytes accessed | tf_op | source)
XLA Modules:
  0.0 130.0 jit_solution(9830155882568192317)
XLA Ops:
  0.0 0.0 copy-start
  0.0 0.0 copy-start.1
  0.0 0.0 copy-start.2
  0.0 1.1 pad_maximum_fusion.1
  1.1 0.0 copy-start.4
  1.1 4.9 %collective-permute-start = (f32[3,2,256]{2,1,0:T(2,128)S(1)}, f32[3,2,256]{2,1,0:T(2,128)S(1)}, u32[]{:S(2)}, u32[]{:S(2)}) collective-permute-start(f32[3,2,256]{2,1,0:T(2,128)S(1)} %slice.95), channel_id=1, source_target_pairs={{0,4},{4,8},{8,12},{12,16},{16,20},{20,24},{24,28},{1,5},{5,9},{9,... | collective-permute-start | bytes 18440 | tf_op jit(solution)/shard_map/ppermute | solution.py:11
  6.1 0.0 copy-done.4
  6.1 0.1 fusion.109
  6.1 0.1 broadcast_multiply_fusion
  6.2 1.2 collective-permute-done
  7.4 0.0 copy-done
  7.4 0.0 copy-done.1
  7.4 0.0 copy-done.2
  7.4 0.1 fusion.12
  7.6 0.0 copy-start.3
  7.6 0.9 copy-done.3
  8.5 0.1 fusion.29
  8.6 0.1 maximum_bitcast_fusion
  8.7 1.5 %copy.53 = f32[2,3,1,128,256]{4,0,2,1,3:T(2,128)} copy(f32[2,3,1,128,256]{4,3,1,0,2:T(8,128)S(1)} %maximum_bitcast_fusion) | data formatting | bytes 1572864 | tf_op jit(solution)/shard_map/broadcast_in_dim | solution.py:48
  10.2 6.6 %all-to-all-start = ((f32[2,3,1,128,256]{4,0,2,1,3:T(2,128)}), f32[2,3,1,128,256]{4,0,2,1,3:T(2,128)S(1)}, u32[]{:S(2)}, u32[]{:S(2)}) async-start(f32[2,3,1,128,256]{4,0,2,1,3:T(2,128)} %copy.53), calls=%async_computation | async-start | bytes 1572864 | tf_op jit(solution)/shard_map/all_to_all | solution.py:51
  16.8 0.1 fusion.82
  16.9 19.0 %all-to-all-done = f32[2,3,1,128,256]{4,0,2,1,3:T(2,128)S(1)} async-done(((f32[2,3,1,128,256]{4,0,2,1,3:T(2,128)}), f32[2,3,1,128,256]{4,0,2,1,3:T(2,128)S(1)}, u32[]{:S(2)}, u32[]{:S(2)}) %all-to-all-start) | async-done | bytes 786464 | tf_op jit(solution)/shard_map/all_to_all | solution.py:51
  35.9 0.1 copy.54
  36.0 0.9 fusion.10
  36.9 0.9 fusion.8
  37.8 0.7 fusion.1
  38.5 0.8 multiply_subtract_fusion
  39.3 1.0 copy.57
  40.3 3.5 %all-to-all-start.1 = ((f32[2,2,8,16,256]{4,3,1,0,2:T(8,128)}), f32[2,2,8,16,256]{4,3,1,0,2:T(8,128)S(1)}, u32[]{:S(2)}, u32[]{:S(2)}) async-start(f32[2,2,8,16,256]{4,3,1,0,2:T(8,128)} %copy.57), calls=%async_computation.1 | async-start | bytes 1048576 | tf_op jit(solution)/shard_map/all_to_all | solution.py:66
  43.8 1.0 copy.60
  44.8 13.4 %all-to-all-done.1 = f32[2,2,8,16,256]{4,3,1,0,2:T(8,128)S(1)} async-done(((f32[2,2,8,16,256]{4,3,1,0,2:T(8,128)}), f32[2,2,8,16,256]{4,3,1,0,2:T(8,128)S(1)}, u32[]{:S(2)}, u32[]{:S(2)}) %all-to-all-start.1) | async-done | bytes 524320 | tf_op jit(solution)/shard_map/all_to_all | solution.py:66
  58.2 3.7 %all-to-all-start.2 = ((f32[2,2,8,16,256]{4,3,1,0,2:T(8,128)}), f32[2,2,8,16,256]{4,3,1,0,2:T(8,128)S(1)}, u32[]{:S(2)}, u32[]{:S(2)}) async-start(f32[2,2,8,16,256]{4,3,1,0,2:T(8,128)} %copy.60), calls=%async_computation.2 | async-start | bytes 1048576 | tf_op jit(solution)/shard_map/all_to_all | solution.py:67
  61.9 0.1 fusion.106
  62.0 1.1 fusion.46
  63.1 13.4 %all-to-all-done.2 = f32[2,2,8,16,256]{4,3,1,0,2:T(8,128)S(1)} async-done(((f32[2,2,8,16,256]{4,3,1,0,2:T(8,128)}), f32[2,2,8,16,256]{4,3,1,0,2:T(8,128)S(1)}, u32[]{:S(2)}, u32[]{:S(2)}) %all-to-all-start.2) | async-done | bytes 524320 | tf_op jit(solution)/shard_map/all_to_all | solution.py:67
  76.5 1.1 fusion.44
  77.6 1.1 fusion.3
  78.8 1.1 fusion.2
  79.9 0.1 multiply_subtract_fusion.1
  80.0 0.6 fusion.14
  80.6 0.6 fusion.18
  81.2 0.6 fusion.6
  81.8 0.6 subtract_bitcast_fusion
  82.5 0.8 copy.65
  83.3 3.6 %all-to-all-start.3 = ((f32[2,1,128,256]{3,0,1,2:T(2,128)}), f32[2,1,128,256]{3,0,1,2:T(2,128)S(1)}, u32[]{:S(2)}, u32[]{:S(2)}) async-start(f32[2,1,128,256]{3,0,1,2:T(2,128)} %copy.65), calls=%async_computation.3 | async-start | bytes 524288 | tf_op jit(solution)/shard_map/all_to_all | solution.py:85
  86.9 0.8 copy.68
  87.8 8.2 %all-to-all-done.3 = f32[2,1,128,256]{3,0,1,2:T(2,128)S(1)} async-done(((f32[2,1,128,256]{3,0,1,2:T(2,128)}), f32[2,1,128,256]{3,0,1,2:T(2,128)S(1)}, u32[]{:S(2)}, u32[]{:S(2)}) %all-to-all-start.3) | async-done | bytes 262176 | tf_op jit(solution)/shard_map/all_to_all | solution.py:85
  96.0 3.6 %all-to-all-start.4 = ((f32[2,1,128,256]{3,0,1,2:T(2,128)}), f32[2,1,128,256]{3,0,1,2:T(2,128)S(1)}, u32[]{:S(2)}, u32[]{:S(2)}) async-start(f32[2,1,128,256]{3,0,1,2:T(2,128)} %copy.68), calls=%async_computation.4 | async-start | bytes 524288 | tf_op jit(solution)/shard_map/all_to_all | solution.py:86
  99.6 0.5 fusion.26
  100.2 8.0 %all-to-all-done.4 = f32[2,1,128,256]{3,0,1,2:T(2,128)S(1)} async-done(((f32[2,1,128,256]{3,0,1,2:T(2,128)}), f32[2,1,128,256]{3,0,1,2:T(2,128)S(1)}, u32[]{:S(2)}, u32[]{:S(2)}) %all-to-all-start.4) | async-done | bytes 262176 | tf_op jit(solution)/shard_map/all_to_all | solution.py:86
  108.2 0.5 fusion.22
  108.7 0.5 fusion.5
  109.3 0.5 fusion.4
  109.9 1.0 copy.73
  110.8 3.6 %all-to-all-start.5 = ((f32[4,8,16,256]{3,2,0,1:T(8,128)}), f32[4,8,16,256]{3,2,0,1:T(8,128)S(1)}, u32[]{:S(2)}, u32[]{:S(2)}) async-start(f32[4,8,16,256]{3,2,0,1:T(8,128)} %copy.73), calls=%async_computation.5 | async-start | bytes 1048576 | tf_op jit(solution)/shard_map/all_to_all | solution.py:91
  114.4 0.1 fusion.108
  114.5 14.1 %all-to-all-done.5 = f32[4,8,16,256]{3,2,0,1:T(8,128)S(1)} async-done(((f32[4,8,16,256]{3,2,0,1:T(8,128)}), f32[4,8,16,256]{3,2,0,1:T(8,128)S(1)}, u32[]{:S(2)}, u32[]{:S(2)}) %all-to-all-start.5) | async-done | bytes 524320 | tf_op jit(solution)/shard_map/all_to_all | solution.py:91
  128.6 0.0 copy-start.5
  128.6 0.7 copy-done.5
  129.2 0.8 fusion.30
  (17 shorter events, 0.4 us)
Async XLA Ops:
  0.0 7.4 %copy-start = (f32[128,256]{1,0:T(8,128)S(1)}, f32[128,256]{1,0:T(8,128)}, u32[]{:S(2)}) copy-start(f32[128,256]{1,0:T(8,128)} %param.8) | copy-start | bytes 393220
  0.0 7.4 %copy-start.1 = (f32[128,256]{1,0:T(8,128)S(1)}, f32[128,256]{1,0:T(8,128)}, u32[]{:S(2)}) copy-start(f32[128,256]{1,0:T(8,128)} %param.7) | copy-start | bytes 393220
  0.0 7.4 %copy-start.2 = (f32[128,256]{1,0:T(8,128)S(1)}, f32[128,256]{1,0:T(8,128)}, u32[]{:S(2)}) copy-start(f32[128,256]{1,0:T(8,128)} %param.6) | copy-start | bytes 393220
  1.1 4.9 %copy-start.4 = (f32[3,256]{1,0:T(4,128)S(1)}, f32[3,256]{1,0:T(4,128)}, u32[]{:S(2)}) copy-start(f32[3,256]{1,0:T(4,128)} %param.10) | copy-start | bytes 9220
  1.1 6.2 %collective-permute-start = (f32[3,2,256]{2,1,0:T(2,128)S(1)}, f32[3,2,256]{2,1,0:T(2,128)S(1)}, u32[]{:S(2)}, u32[]{:S(2)}) collective-permute-start(f32[3,2,256]{2,1,0:T(2,128)S(1)} %slice.95), channel_id=1, source_target_pairs={{0,4},{4,8},{8,12},{12,16},{16,20},{20,24},{24,28},{1,5},{5,9},{9,... | collective-permute-start | bytes 18440 | tf_op jit(solution)/shard_map/ppermute | solution.py:11
  7.6 0.9 copy-start.3
  10.2 25.7 %all-to-all-start = ((f32[2,3,1,128,256]{4,0,2,1,3:T(2,128)}), f32[2,3,1,128,256]{4,0,2,1,3:T(2,128)S(1)}, u32[]{:S(2)}, u32[]{:S(2)}) async-start(f32[2,3,1,128,256]{4,0,2,1,3:T(2,128)} %copy.53), calls=%async_computation | async-start | bytes 1572864 | tf_op jit(solution)/shard_map/all_to_all | solution.py:51
  40.3 17.9 %all-to-all-start.1 = ((f32[2,2,8,16,256]{4,3,1,0,2:T(8,128)}), f32[2,2,8,16,256]{4,3,1,0,2:T(8,128)S(1)}, u32[]{:S(2)}, u32[]{:S(2)}) async-start(f32[2,2,8,16,256]{4,3,1,0,2:T(8,128)} %copy.57), calls=%async_computation.1 | async-start | bytes 1048576 | tf_op jit(solution)/shard_map/all_to_all | solution.py:66
  58.2 18.3 %all-to-all-start.2 = ((f32[2,2,8,16,256]{4,3,1,0,2:T(8,128)}), f32[2,2,8,16,256]{4,3,1,0,2:T(8,128)S(1)}, u32[]{:S(2)}, u32[]{:S(2)}) async-start(f32[2,2,8,16,256]{4,3,1,0,2:T(8,128)} %copy.60), calls=%async_computation.2 | async-start | bytes 1048576 | tf_op jit(solution)/shard_map/all_to_all | solution.py:67
  83.3 12.7 %all-to-all-start.3 = ((f32[2,1,128,256]{3,0,1,2:T(2,128)}), f32[2,1,128,256]{3,0,1,2:T(2,128)S(1)}, u32[]{:S(2)}, u32[]{:S(2)}) async-start(f32[2,1,128,256]{3,0,1,2:T(2,128)} %copy.65), calls=%async_computation.3 | async-start | bytes 524288 | tf_op jit(solution)/shard_map/all_to_all | solution.py:85
  96.0 12.2 %all-to-all-start.4 = ((f32[2,1,128,256]{3,0,1,2:T(2,128)}), f32[2,1,128,256]{3,0,1,2:T(2,128)S(1)}, u32[]{:S(2)}, u32[]{:S(2)}) async-start(f32[2,1,128,256]{3,0,1,2:T(2,128)} %copy.68), calls=%async_computation.4 | async-start | bytes 524288 | tf_op jit(solution)/shard_map/all_to_all | solution.py:86
  110.8 17.7 %all-to-all-start.5 = ((f32[4,8,16,256]{3,2,0,1:T(8,128)}), f32[4,8,16,256]{3,2,0,1:T(8,128)S(1)}, u32[]{:S(2)}, u32[]{:S(2)}) async-start(f32[4,8,16,256]{3,2,0,1:T(8,128)} %copy.73), calls=%async_computation.5 | async-start | bytes 1048576 | tf_op jit(solution)/shard_map/all_to_all | solution.py:91
  128.6 0.7 copy-start.5
where the time goes:
time: 131 us; the launch traced here: 130 us
  waiting for transfers between devices  77.2 us (59%)
  starting transfers between devices  29.5 us (23%)
  matrix products  12.3 us (9%)
  local copies, waits for them, and re-layouts  7.97 us (6%)
  other arithmetic  2.65 us (2%)
    all_to_all x1, waiting for transfers between devices, body(): lax.all_to_all(lifted, 'seq', split_axis=3, concat_axis=2, tiled=True)  19 us
    all_to_all x1, waiting for transfers between devices, body(): lax.all_to_all(packed, 'seq', split_axis=1, concat_axis=2, tiled=True)  14.1 us
    all_to_all x1, waiting for transfers between devices, body(): lax.all_to_all(real_part, 'seq', split_axis=2, concat_axis=3, tiled=True)  13.4 us
    all_to_all x1, waiting for transfers between devices, body(): lax.all_to_all(imag_part, 'seq', split_axis=2, concat_axis=3, tiled=True)  13.4 us
    all_to_all x1, waiting for transfers between devices, body(): lax.all_to_all(back_real, 'seq', split_axis=2, concat_axis=1, tiled=True)  8.24 us
    all_to_all x1, waiting for transfers between devices, body(): lax.all_to_all(back_imag, 'seq', split_axis=2, concat_axis=1, tiled=True)  8.02 us
    all_to_all x1, starting transfers between devices, body(): lax.all_to_all(lifted, 'seq', split_axis=3, concat_axis=2, tiled=True)  6.6 us
    ppermute x1, starting transfers between devices, passed_along(): return lax.ppermute(block, axis, route)  4.9 us
  transfers between devices with their start and end apart: 7, of which 7 were waited for; matrix products, arithmetic and copies ran while one was open for 3% of the time, Pallas kernels for 0%

commit v1 on v0

--- a/solution.py
+++ b/solution.py
@@ -1,8 +1,36 @@
+import functools
 import math
 import jax
 import jax.numpy as jnp
 from jax import lax
 from jax.sharding import PartitionSpec as P
+
+
+def watch_side_over_axis(field, join_dim, load):
+    known, newest = (field.shape[:join_dim], field.shape[join_dim + 1 :])
+    return jnp.moveaxis(field.reshape(*known, load, -1, *newest), join_dim, 0)
+
+
+def write_table(vals, in_dim):
+    y = list(vals.shape[1:])
+    y[in_dim] *= vals.shape[0]
+    return jnp.moveaxis(vals, 0, in_dim).reshape(y)
+
+
+def _fit_shapes(local_x, along_axis, arr_in, state):
+    parts_out, before = (lax.axis_size(along_axis), lax.axis_index(along_axis))
+    tall = watch_side_over_axis(local_x, arr_in, parts_out)
+    xs_all = [tall[before]]
+    for q in range(1, parts_out):
+        y_new = tall[(before + q) % parts_out]
+        xs_all.append(
+            lax.ppermute(y_new, along_axis, [(w, (w + q) % parts_out) for w in range(parts_out)])
+        )
+    tall = jnp.stack(xs_all)[(before - jnp.arange(parts_out)) % parts_out]
+    return write_table(tall, state)
+
+
+fit_circles = functools.partial(_fit_shapes, along_axis="seq", arr_in=2, state=1)
 
 
 def passed_along(block, axis, distance):
@@ -83,7 +111,7 @@
     column_cos, column_sin = angles(column_index[:, None] * column_index[None, :], shards, 1.0)
     pair = (
         lax.all_to_all(back_real, "seq", split_axis=2, concat_axis=1, tiled=True),
-        lax.all_to_all(back_imag, "seq", split_axis=2, concat_axis=1, tiled=True),
+        fit_circles(back_imag),
     )
     inv_real, inv_imag = complex_mix("dk,rkmc->rdmc", column_cos, column_sin, pair[0], pair[1])
     factor = 0.5 / total

time: 131 us -> 125 us (0.954)
  waiting for transfers between devices: 77.2 us -> 60.1 us
  starting transfers between devices: 29.5 us -> 40.4 us
    ppermute x0 -> x7, starting transfers between devices: none -> 12.6 us  [_fit_shapes(): lax.ppermute(y_new, along_axis, [(w, (w + q) % parts_out) for w in range(...]
    all_to_all x1, waiting for transfers between devices: 8.24 us -> 0.01 us  [body(): lax.all_to_all(back_real, 'seq', split_axis=2, concat_axis=1, tiled=True)]
    all_to_all x1 -> x0, waiting for transfers between devices: 8.02 us -> none  [body(): lax.all_to_all(back_imag, 'seq', split_axis=2, concat_axis=1, tiled=True)]
    all_to_all x1 -> x0, starting transfers between devices: 3.59 us -> none  [body(): lax.all_to_all(back_imag, 'seq', split_axis=2, concat_axis=1, tiled=True)]
    all_to_all x1, waiting for transfers between devices: 14.1 us -> 11.6 us  [body(): lax.all_to_all(packed, 'seq', split_axis=1, concat_axis=2, tiled=True)]
    ppermute x0 -> x7, waiting for transfers between devices: none -> 2.4 us  [_fit_shapes(): lax.ppermute(y_new, along_axis, [(w, (w + q) % parts_out) for w in range(...]
    all_to_all x1, starting transfers between devices: 3.59 us -> 5.43 us  [body(): lax.all_to_all(packed, 'seq', split_axis=1, concat_axis=2, tiled=True)]
  transfers between devices with their start and end apart: 7 -> 13, of which waited for: 7 -> 7; matrix products, arithmetic and copies ran while one was open for 3% -> 4% of each run, Pallas kernels for 0% -> 0%
where the time goes in v1:
time: 125 us
  waiting for transfers between devices  60.1 us (48%)
  starting transfers between devices  40.4 us (32%)
  matrix products  12.4 us (10%)
  local copies, waits for them, and re-layouts  8.37 us (7%)
  other arithmetic  2.67 us (2%)
    all_to_all x1, waiting for transfers between devices, body(): lax.all_to_all(lifted, 'seq', split_axis=3, concat_axis=2, tiled=True)  19 us
    all_to_all x1, waiting for transfers between devices, body(): lax.all_to_all(real_part, 'seq', split_axis=2, concat_axis=3, tiled=True)  13.4 us
    all_to_all x1, waiting for transfers between devices, body(): lax.all_to_all(imag_part, 'seq', split_axis=2, concat_axis=3, tiled=True)  13.2 us
    ppermute x7, starting transfers between devices, _fit_shapes(): lax.ppermute(y_new, along_axis, [(w, (w + q) % parts_out) for w in range(...  12.6 us
    all_to_all x1, waiting for transfers between devices, body(): lax.all_to_all(packed, 'seq', split_axis=1, concat_axis=2, tiled=True)  11.6 us
    all_to_all x1, starting transfers between devices, body(): lax.all_to_all(lifted, 'seq', split_axis=3, concat_axis=2, tiled=True)  6.6 us
    all_to_all x1, starting transfers between devices, body(): lax.all_to_all(packed, 'seq', split_axis=1, concat_axis=2, tiled=True)  5.43 us
    ppermute x1, starting transfers between devices, passed_along(): return lax.ppermute(block, axis, route)  4.9 us
  transfers between devices with their start and end apart: 13, of which 7 were waited for; matrix products, arithmetic and copies ran while one was open for 4% of the time, Pallas kernels for 0%

profile of v1, /device:TPU:0, one launch (start us, length us, event | category | flops | bytes accessed | tf_op | source)
XLA Modules:
  0.0 124.5 jit_solution(10978525015470905914)
XLA Ops:
  0.0 1.1 pad_maximum_fusion.1
  1.1 4.9 %collective-permute-start = (f32[3,2,256]{2,1,0:T(2,128)S(1)}, f32[3,2,256]{2,1,0:T(2,128)S(1)}, u32[]{:S(2)}, u32[]{:S(2)}) collective-permute-start(f32[3,2,256]{2,1,0:T(2,128)S(1)} %slice.97), channel_id=1, source_target_pairs={{0,4},{4,8},{8,12},{12,16},{16,20},{20,24},{24,28},{1,5},{5,9},{9,... | collective-permute-start | bytes 18440 | tf_op jit(solution)/shard_map/ppermute | solution.py:39
  6.0 0.0 copy-start.4
  6.1 0.1 broadcast_multiply_fusion
  6.1 0.6 copy-done.4
  6.7 0.1 fusion.127
  6.8 0.6 collective-permute-done
  7.4 0.1 fusion.12
  7.5 0.0 copy-start.3
  7.6 0.9 copy-done.3
  8.5 0.1 fusion.29
  8.6 0.1 maximum_bitcast_fusion
  8.6 1.5 %copy.82 = f32[2,3,1,128,256]{4,0,2,1,3:T(2,128)} copy(f32[2,3,1,128,256]{4,3,1,0,2:T(8,128)S(1)} %maximum_bitcast_fusion) | data formatting | bytes 1572864 | tf_op jit(solution)/shard_map/broadcast_in_dim | solution.py:76
  10.2 6.6 %all-to-all-start = ((f32[2,3,1,128,256]{4,0,2,1,3:T(2,128)}), f32[2,3,1,128,256]{4,0,2,1,3:T(2,128)S(1)}, u32[]{:S(2)}, u32[]{:S(2)}) async-start(f32[2,3,1,128,256]{4,0,2,1,3:T(2,128)} %copy.82), calls=%async_computation | async-start | bytes 1572864 | tf_op jit(solution)/shard_map/all_to_all | solution.py:79
  16.8 0.1 fusion.82
  16.9 19.0 %all-to-all-done = f32[2,3,1,128,256]{4,0,2,1,3:T(2,128)S(1)} async-done(((f32[2,3,1,128,256]{4,0,2,1,3:T(2,128)}), f32[2,3,1,128,256]{4,0,2,1,3:T(2,128)S(1)}, u32[]{:S(2)}, u32[]{:S(2)}) %all-to-all-start) | async-done | bytes 786464 | tf_op jit(solution)/shard_map/all_to_all | solution.py:79
  35.9 0.1 copy.83
  36.0 0.9 fusion.10
  36.9 0.9 fusion.8
  37.8 0.7 fusion.1
  38.5 0.8 multiply_subtract_fusion
  39.3 1.0 copy.86
  40.3 3.5 %all-to-all-start.1 = ((f32[2,2,8,16,256]{4,3,1,0,2:T(8,128)}), f32[2,2,8,16,256]{4,3,1,0,2:T(8,128)S(1)}, u32[]{:S(2)}, u32[]{:S(2)}) async-start(f32[2,2,8,16,256]{4,3,1,0,2:T(8,128)} %copy.86), calls=%async_computation.1 | async-start | bytes 1048576 | tf_op jit(solution)/shard_map/all_to_all | solution.py:94
  43.8 1.0 copy.89
  44.8 13.4 %all-to-all-done.1 = f32[2,2,8,16,256]{4,3,1,0,2:T(8,128)S(1)} async-done(((f32[2,2,8,16,256]{4,3,1,0,2:T(8,128)}), f32[2,2,8,16,256]{4,3,1,0,2:T(8,128)S(1)}, u32[]{:S(2)}, u32[]{:S(2)}) %all-to-all-start.1) | async-done | bytes 524320 | tf_op jit(solution)/shard_map/all_to_all | solution.py:94
  58.2 3.7 %all-to-all-start.2 = ((f32[2,2,8,16,256]{4,3,1,0,2:T(8,128)}), f32[2,2,8,16,256]{4,3,1,0,2:T(8,128)S(1)}, u32[]{:S(2)}, u32[]{:S(2)}) async-start(f32[2,2,8,16,256]{4,3,1,0,2:T(8,128)} %copy.89), calls=%async_computation.2 | async-start | bytes 1048576 | tf_op jit(solution)/shard_map/all_to_all | solution.py:95
  61.9 0.1 fusion.125
  62.1 1.1 fusion.46
  63.2 13.2 %all-to-all-done.2 = f32[2,2,8,16,256]{4,3,1,0,2:T(8,128)S(1)} async-done(((f32[2,2,8,16,256]{4,3,1,0,2:T(8,128)}), f32[2,2,8,16,256]{4,3,1,0,2:T(8,128)S(1)}, u32[]{:S(2)}, u32[]{:S(2)}) %all-to-all-start.2) | async-done | bytes 524320 | tf_op jit(solution)/shard_map/all_to_all | solution.py:95
  76.5 1.1 fusion.44
  77.6 1.1 fusion.3
  78.7 1.1 fusion.2
  79.9 0.1 multiply_subtract_fusion.1
  79.9 0.6 fusion.14
  80.6 0.6 fusion.18
  81.2 0.6 fusion.6
  81.9 0.7 subtract_bitcast_fusion
  82.6 1.5 %collective-permute-start.1 = (f32[2,1,16,256]{3,2,0,1:T(8,128)S(1)}, f32[2,1,16,256]{3,2,0,1:T(8,128)S(1)}, u32[]{:S(2)}, u32[]{:S(2)}) collective-permute-start(f32[2,1,16,256]{3,2,0,1:T(8,128)S(1)} %get-tuple-element.24), channel_id=1, source_target_pairs={{0,4},{4,8},{8,12},{12,16},{16,20},{20,24},{24,28},{28,0},{1,5},{5... | collective-permute-start | bytes 98312 | tf_op jit(solution)/shard_map/ppermute | solution.py:27
  84.1 0.0 collective-permute-start.2
  84.1 1.8 %collective-permute-start.3 = (f32[2,1,16,256]{3,2,0,1:T(8,128)S(1)}, f32[2,1,16,256]{3,2,0,1:T(8,128)S(1)}, u32[]{:S(2)}, u32[]{:S(2)}) collective-permute-start(f32[2,1,16,256]{3,2,0,1:T(8,128)S(1)} %get-tuple-element.22), channel_id=1, source_target_pairs={{0,12},{4,16},{8,20},{12,24},{16,28},{20,0},{24,4},{28,8},{1,13},{... | collective-permute-start | bytes 98312 | tf_op jit(solution)/shard_map/ppermute | solution.py:27
  85.9 2.8 %collective-permute-start.4 = (f32[2,1,16,256]{3,2,0,1:T(8,128)S(1)}, f32[2,1,16,256]{3,2,0,1:T(8,128)S(1)}, u32[]{:S(2)}, u32[]{:S(2)}) collective-permute-start(f32[2,1,16,256]{3,2,0,1:T(8,128)S(1)} %get-tuple-element.21), channel_id=1, source_target_pairs={{0,16},{4,20},{8,24},{12,28},{16,0},{20,4},{24,8},{28,12},{1,17},{... | collective-permute-start | bytes 98312 | tf_op jit(solution)/shard_map/ppermute | solution.py:27
  88.7 1.3 %collective-permute-start.5 = (f32[2,1,16,256]{3,2,0,1:T(8,128)S(1)}, f32[2,1,16,256]{3,2,0,1:T(8,128)S(1)}, u32[]{:S(2)}, u32[]{:S(2)}) collective-permute-start(f32[2,1,16,256]{3,2,0,1:T(8,128)S(1)} %get-tuple-element.20), channel_id=1, source_target_pairs={{0,20},{4,24},{8,28},{12,0},{16,4},{20,8},{24,12},{28,16},{1,21},{... | collective-permute-start | bytes 98312 | tf_op jit(solution)/shard_map/ppermute | solution.py:27
  90.0 0.9 copy.98
  90.9 3.6 %all-to-all-start.3 = ((f32[2,1,128,256]{3,0,1,2:T(2,128)}), f32[2,1,128,256]{3,0,1,2:T(2,128)S(1)}, u32[]{:S(2)}, u32[]{:S(2)}) async-start(f32[2,1,128,256]{3,0,1,2:T(2,128)} %copy.98), calls=%async_computation.3 | async-start | bytes 524288 | tf_op jit(solution)/shard_map/all_to_all | solution.py:113
  94.5 0.0 collective-permute-done.1
  94.5 3.8 %collective-permute-start.6 = (f32[2,1,16,256]{3,2,0,1:T(8,128)S(1)}, f32[2,1,16,256]{3,2,0,1:T(8,128)S(1)}, u32[]{:S(2)}, u32[]{:S(2)}) collective-permute-start(f32[2,1,16,256]{3,2,0,1:T(8,128)S(1)} %get-tuple-element.19), channel_id=1, source_target_pairs={{0,24},{4,28},{8,0},{12,4},{16,8},{20,12},{24,16},{28,20},{1,25},{... | collective-permute-start | bytes 98312 | tf_op jit(solution)/shard_map/ppermute | solution.py:27
  98.3 0.0 collective-permute-done.2
  98.3 1.5 %collective-permute-start.7 = (f32[2,1,16,256]{3,2,0,1:T(8,128)S(1)}, f32[2,1,16,256]{3,2,0,1:T(8,128)S(1)}, u32[]{:S(2)}, u32[]{:S(2)}) collective-permute-start(f32[2,1,16,256]{3,2,0,1:T(8,128)S(1)} %get-tuple-element.18), channel_id=1, source_target_pairs={{0,28},{4,0},{8,4},{12,8},{16,12},{20,16},{24,20},{28,24},{1,29},{... | collective-permute-start | bytes 98312 | tf_op jit(solution)/shard_map/ppermute | solution.py:27
  99.8 0.0 collective-permute-done.3
  99.8 0.0 collective-permute-done.4
  99.9 0.1 collective-permute-done.6
  99.9 2.3 %collective-permute-done.7 = f32[2,1,16,256]{3,2,0,1:T(8,128)S(1)} collective-permute-done((f32[2,1,16,256]{3,2,0,1:T(8,128)S(1)}, f32[2,1,16,256]{3,2,0,1:T(8,128)S(1)}, u32[]{:S(2)}, u32[]{:S(2)}) %collective-permute-start.7) | collective-permute-done | bytes 32800 | tf_op jit(solution)/shard_map/ppermute | solution.py:27
  102.3 0.6 gather_fusion
  102.8 0.5 fusion.22
  103.4 0.5 fusion.26
  103.9 0.5 fusion.5
  104.5 0.5 fusion.4
  105.0 1.0 copy.104
  106.0 5.4 %all-to-all-start.4 = ((f32[4,8,16,256]{3,2,0,1:T(8,128)}), f32[4,8,16,256]{3,2,0,1:T(8,128)S(1)}, u32[]{:S(2)}, u32[]{:S(2)}) async-start(f32[4,8,16,256]{3,2,0,1:T(8,128)} %copy.104), calls=%async_computation.4 | async-start | bytes 1048576 | tf_op jit(solution)/shard_map/all_to_all | solution.py:119
  111.4 0.1 fusion.126
  111.5 11.6 %all-to-all-done.4 = f32[4,8,16,256]{3,2,0,1:T(8,128)S(1)} async-done(((f32[4,8,16,256]{3,2,0,1:T(8,128)}), f32[4,8,16,256]{3,2,0,1:T(8,128)S(1)}, u32[]{:S(2)}, u32[]{:S(2)}) %all-to-all-start.4) | async-done | bytes 524320 | tf_op jit(solution)/shard_map/all_to_all | solution.py:119
  123.1 0.0 copy-start.5
  123.1 0.7 copy-done.5
  123.8 0.8 fusion.30
  (35 shorter events, 0.4 us)
Async XLA Ops:
  0.0 7.4 %copy-start = (f32[128,256]{1,0:T(8,128)S(1)}, f32[128,256]{1,0:T(8,128)}, u32[]{:S(2)}) copy-start(f32[128,256]{1,0:T(8,128)} %param.8) | copy-start | bytes 393220
  0.0 7.4 %copy-start.1 = (f32[128,256]{1,0:T(8,128)S(1)}, f32[128,256]{1,0:T(8,128)}, u32[]{:S(2)}) copy-start(f32[128,256]{1,0:T(8,128)} %param.7) | copy-start | bytes 393220
  0.0 7.4 %copy-start.2 = (f32[128,256]{1,0:T(8,128)S(1)}, f32[128,256]{1,0:T(8,128)}, u32[]{:S(2)}) copy-start(f32[128,256]{1,0:T(8,128)} %param.6) | copy-start | bytes 393220
  1.1 6.2 %collective-permute-start = (f32[3,2,256]{2,1,0:T(2,128)S(1)}, f32[3,2,256]{2,1,0:T(2,128)S(1)}, u32[]{:S(2)}, u32[]{:S(2)}) collective-permute-start(f32[3,2,256]{2,1,0:T(2,128)S(1)} %slice.97), channel_id=1, source_target_pairs={{0,4},{4,8},{8,12},{12,16},{16,20},{20,24},{24,28},{1,5},{5,9},{9,... | collective-permute-start | bytes 18440 | tf_op jit(solution)/shard_map/ppermute | solution.py:39
  6.0 0.7 copy-start.4
  7.5 0.9 copy-start.3
  10.2 25.7 %all-to-all-start = ((f32[2,3,1,128,256]{4,0,2,1,3:T(2,128)}), f32[2,3,1,128,256]{4,0,2,1,3:T(2,128)S(1)}, u32[]{:S(2)}, u32[]{:S(2)}) async-start(f32[2,3,1,128,256]{4,0,2,1,3:T(2,128)} %copy.82), calls=%async_computation | async-start | bytes 1572864 | tf_op jit(solution)/shard_map/all_to_all | solution.py:79
  40.3 17.9 %all-to-all-start.1 = ((f32[2,2,8,16,256]{4,3,1,0,2:T(8,128)}), f32[2,2,8,16,256]{4,3,1,0,2:T(8,128)S(1)}, u32[]{:S(2)}, u32[]{:S(2)}) async-start(f32[2,2,8,16,256]{4,3,1,0,2:T(8,128)} %copy.86), calls=%async_computation.1 | async-start | bytes 1048576 | tf_op jit(solution)/shard_map/all_to_all | solution.py:94
  58.2 18.3 %all-to-all-start.2 = ((f32[2,2,8,16,256]{4,3,1,0,2:T(8,128)}), f32[2,2,8,16,256]{4,3,1,0,2:T(8,128)S(1)}, u32[]{:S(2)}, u32[]{:S(2)}) async-start(f32[2,2,8,16,256]{4,3,1,0,2:T(8,128)} %copy.89), calls=%async_computation.2 | async-start | bytes 1048576 | tf_op jit(solution)/shard_map/all_to_all | solution.py:95
  82.6 11.9 %collective-permute-start.1 = (f32[2,1,16,256]{3,2,0,1:T(8,128)S(1)}, f32[2,1,16,256]{3,2,0,1:T(8,128)S(1)}, u32[]{:S(2)}, u32[]{:S(2)}) collective-permute-start(f32[2,1,16,256]{3,2,0,1:T(8,128)S(1)} %get-tuple-element.24), channel_id=1, source_target_pairs={{0,4},{4,8},{8,12},{12,16},{16,20},{20,24},{24,28},{28,0},{1,5},{5... | collective-permute-start | bytes 98312 | tf_op jit(solution)/shard_map/ppermute | solution.py:27
  84.1 14.2 %collective-permute-start.2 = (f32[2,1,16,256]{3,2,0,1:T(8,128)S(1)}, f32[2,1,16,256]{3,2,0,1:T(8,128)S(1)}, u32[]{:S(2)}, u32[]{:S(2)}) collective-permute-start(f32[2,1,16,256]{3,2,0,1:T(8,128)S(1)} %get-tuple-element.23), channel_id=1, source_target_pairs={{0,8},{4,12},{8,16},{12,20},{16,24},{20,28},{24,0},{28,4},{1,9},{5... | collective-permute-start | bytes 98312 | tf_op jit(solution)/shard_map/ppermute | solution.py:27
  84.1 15.7 %collective-permute-start.3 = (f32[2,1,16,256]{3,2,0,1:T(8,128)S(1)}, f32[2,1,16,256]{3,2,0,1:T(8,128)S(1)}, u32[]{:S(2)}, u32[]{:S(2)}) collective-permute-start(f32[2,1,16,256]{3,2,0,1:T(8,128)S(1)} %get-tuple-element.22), channel_id=1, source_target_pairs={{0,12},{4,16},{8,20},{12,24},{16,28},{20,0},{24,4},{28,8},{1,13},{... | collective-permute-start | bytes 98312 | tf_op jit(solution)/shard_map/ppermute | solution.py:27
  85.9 13.9 %collective-permute-start.4 = (f32[2,1,16,256]{3,2,0,1:T(8,128)S(1)}, f32[2,1,16,256]{3,2,0,1:T(8,128)S(1)}, u32[]{:S(2)}, u32[]{:S(2)}) collective-permute-start(f32[2,1,16,256]{3,2,0,1:T(8,128)S(1)} %get-tuple-element.21), channel_id=1, source_target_pairs={{0,16},{4,20},{8,24},{12,28},{16,0},{20,4},{24,8},{28,12},{1,17},{... | collective-permute-start | bytes 98312 | tf_op jit(solution)/shard_map/ppermute | solution.py:27
  88.7 11.1 %collective-permute-start.5 = (f32[2,1,16,256]{3,2,0,1:T(8,128)S(1)}, f32[2,1,16,256]{3,2,0,1:T(8,128)S(1)}, u32[]{:S(2)}, u32[]{:S(2)}) collective-permute-start(f32[2,1,16,256]{3,2,0,1:T(8,128)S(1)} %get-tuple-element.20), channel_id=1, source_target_pairs={{0,20},{4,24},{8,28},{12,0},{16,4},{20,8},{24,12},{28,16},{1,21},{... | collective-permute-start | bytes 98312 | tf_op jit(solution)/shard_map/ppermute | solution.py:27
  90.9 12.5 %all-to-all-start.3 = ((f32[2,1,128,256]{3,0,1,2:T(2,128)}), f32[2,1,128,256]{3,0,1,2:T(2,128)S(1)}, u32[]{:S(2)}, u32[]{:S(2)}) async-start(f32[2,1,128,256]{3,0,1,2:T(2,128)} %copy.98), calls=%async_computation.3 | async-start | bytes 524288 | tf_op jit(solution)/shard_map/all_to_all | solution.py:113
  94.5 5.4 %collective-permute-start.6 = (f32[2,1,16,256]{3,2,0,1:T(8,128)S(1)}, f32[2,1,16,256]{3,2,0,1:T(8,128)S(1)}, u32[]{:S(2)}, u32[]{:S(2)}) collective-permute-start(f32[2,1,16,256]{3,2,0,1:T(8,128)S(1)} %get-tuple-element.19), channel_id=1, source_target_pairs={{0,24},{4,28},{8,0},{12,4},{16,8},{20,12},{24,16},{28,20},{1,25},{... | collective-permute-start | bytes 98312 | tf_op jit(solution)/shard_map/ppermute | solution.py:27
  98.3 3.9 %collective-permute-start.7 = (f32[2,1,16,256]{3,2,0,1:T(8,128)S(1)}, f32[2,1,16,256]{3,2,0,1:T(8,128)S(1)}, u32[]{:S(2)}, u32[]{:S(2)}) collective-permute-start(f32[2,1,16,256]{3,2,0,1:T(8,128)S(1)} %get-tuple-element.18), channel_id=1, source_target_pairs={{0,28},{4,0},{8,4},{12,8},{16,12},{20,16},{24,20},{28,24},{1,29},{... | collective-permute-start | bytes 98312 | tf_op jit(solution)/shard_map/ppermute | solution.py:27
  106.0 17.0 %all-to-all-start.4 = ((f32[4,8,16,256]{3,2,0,1:T(8,128)}), f32[4,8,16,256]{3,2,0,1:T(8,128)S(1)}, u32[]{:S(2)}, u32[]{:S(2)}) async-start(f32[4,8,16,256]{3,2,0,1:T(8,128)} %copy.104), calls=%async_computation.4 | async-start | bytes 1048576 | tf_op jit(solution)/shard_map/all_to_all | solution.py:119
  123.1 0.7 copy-start.5
